TPU v7x, 128 devices: a whole 4x4x4 slice. The times are simulated.
128 devices in a mesh: sec: 2 (over core), dev: 64 (over z, x, y).
Axes of the slice: x: 4, y: 4, z: 4, core: 2. Of those that a mesh axis runs over, the one named last changes fastest.
Arguments:
- queries: bfloat16 [256, 4, 6144], P('dev'), may hold values from -160 to 160
- cache_keys: bfloat16 [256, 128, 1024], P('dev'), may hold values from -8 to 8
- cache_values: bfloat16 [256, 128, 1024], P('dev'), may hold values from -6 to 6
- lengths: int32 [256], P('dev'), may hold values from 1 to 128, 16384 in all
- new_keys: bfloat16 [256, 4, 1024], P('dev'), may hold values from -6 to 6
- new_values: bfloat16 [256, 4, 1024], P('dev'), may hold values from -6 to 6
- residual: bfloat16 [256, 4, 6144], P('dev'), may hold values from -6 to 6
- norm_gain: float32 [6144], replicated, may hold values from 0.25 to 1.75
- expert_ids: int32 [1024, 2], P('dev'), may hold values from 0 to 3, all different within a row; in each aligned block of 16 rows (0 to 15, 16 to 31, ...) at most 9 rows name the same one
- gate_logits: float32 [1024, 2], P('dev'), may hold values from -8 to 8
- w_gate: bfloat16 [6144, 32768], P(None, 'dev'), may hold values from -0.078125 to 0.078125
- w_up: bfloat16 [6144, 32768], P(None, 'dev'), may hold values from -0.078125 to 0.078125
- w_down: bfloat16 [32768, 6144], P('dev'), may hold values from -0.0625 to 0.0625
Outputs:
- layer_out: bfloat16 [256, 4, 6144], P('dev', None, 'sec')
Inputs may be any that keep to these rules, and one draw needn't show every extreme that they name: `expert_ids`: in the 16 tokens of one attention device no expert is named more than 9 times; some expert is named exactly 9 times in some of these blocks.
All inputs are finite; a program needn't handle non-finite values. No bound on the sum of `lengths` on one device may be relied on, other than what follows from the above.
Results may differ from a plain program's by a relative error of at most 0.0065.
Values may be sent and summed in bfloat16 or wider, within the bound.
A program may use at most 192 MiB of HBM per device.

v0:
```python
import jax
import jax.numpy as jnp
from jax import lax
from jax.sharding import PartitionSpec as P

HEADS = 48
KVH = 8
HD = 128
EXP = 4
LMAX = 128
CAP = 9
epsilon = 1e-05


def from_behind(x, axis, by):
    size = lax.axis_size(axis)
    pairs = [(i, i + by) for i in range(size) if 0 <= i + by < size]
    return lax.ppermute(x, axis, pairs)


def attend_local(operands):
    queries, cache_keys, cache_values, lengths, new_keys, new_values, residual, norm_gain = operands
    requests = queries.shape[0]
    steps = queries.shape[1]
    width = residual.shape[2]
    per_group = HEADS // KVH
    key_all = jnp.concatenate([cache_keys, new_keys], axis=1).reshape(
        requests, LMAX + steps, KVH, HD
    )
    value_all = jnp.concatenate([cache_values, new_values], axis=1).reshape(
        requests, LMAX + steps, KVH, HD
    )
    query_heads = queries.reshape(requests, steps, KVH, per_group, HD)
    scores = jnp.einsum(
        "rsgqd,rlgd->rsgql", query_heads, key_all, preferred_element_type=jnp.float32
    ) * HD ** (-0.5)
    position = jnp.arange(LMAX + steps, dtype=jnp.int32)
    stepnum = jnp.arange(steps, dtype=jnp.int32)
    in_cache = position[None, None, :] < lengths[:, None, None]
    in_window = (position[None, :] >= LMAX) & (position[None, :] - LMAX <= stepnum[:, None])
    valid = in_cache | in_window[None, :, :]
    scores = jnp.where(valid[:, :, None, None, :], scores, jnp.float32(-1e30))
    peak = jnp.max(scores, axis=-1, keepdims=True)
    expo = jnp.exp(scores - peak)
    probs = (expo / jnp.sum(expo, axis=-1, keepdims=True)).astype(jnp.bfloat16)
    attended = jnp.einsum("rsgql,rlgd->rsgqd", probs, value_all, preferred_element_type=jnp.float32)
    attended = attended.reshape(requests, steps, width)
    hstate = (residual.astype(jnp.float32) + attended).astype(jnp.bfloat16)
    hfloat = hstate.astype(jnp.float32)
    meansq = jnp.mean(hfloat * hfloat, axis=-1, keepdims=True)
    normed = (hfloat * lax.rsqrt(meansq + epsilon) * norm_gain).astype(jnp.bfloat16)
    return (hstate, normed)


def attend_skip(operands):
    residual = operands[6]
    return (jnp.zeros_like(residual), jnp.zeros_like(residual))


def expert_rows(rows, w_gate, w_up, w_down):
    gate = jnp.dot(rows, w_gate, preferred_element_type=jnp.float32)
    upward = jnp.dot(rows, w_up, preferred_element_type=jnp.float32)
    hidden = (jax.nn.silu(gate) * upward).astype(jnp.bfloat16)
    return jnp.dot(hidden, w_down, preferred_element_type=jnp.float32).astype(jnp.bfloat16)


def shards(
    queries,
    cache_keys,
    cache_values,
    lengths,
    new_keys,
    new_values,
    residual,
    norm_gain,
    expert_ids,
    gate_logits,
    w_gate,
    w_up,
    w_down,
):
    is_attention = lax.axis_index("sec") == 0
    is_expert = jnp.logical_not(is_attention)
    devices = lax.axis_size("dev")
    group = devices // EXP
    my_expert = lax.axis_index("dev") // group
    requests = residual.shape[0]
    steps = residual.shape[1]
    width = residual.shape[2]
    half = width // 2
    tok_rows = requests * steps
    operands = (
        queries,
        cache_keys,
        cache_values,
        lengths,
        new_keys,
        new_values,
        residual,
        norm_gain,
    )
    hstate, normed = lax.cond(is_attention, attend_local, attend_skip, operands)
    flat_h = hstate.reshape(tok_rows, width)
    flat_in = normed.reshape(tok_rows, width)
    flat_ids = expert_ids.reshape(-1)
    onehot = (flat_ids[:, None] == jnp.arange(EXP, dtype=jnp.int32)[None, :]).astype(jnp.int32)
    ranks = jnp.cumsum(onehot, axis=0) - onehot
    slot_of = jnp.sum(ranks * onehot, axis=1)
    target = (flat_ids * CAP + slot_of).reshape(tok_rows, 2)
    slot_rows = jnp.arange(EXP * CAP, dtype=jnp.int32)
    first_hit = target[:, 0:1] == slot_rows[None, :]
    second_hit = target[:, 1:2] == slot_rows[None, :]
    placing = jnp.logical_or(first_hit, second_hit).astype(jnp.bfloat16)
    buffer = lax.dot_general(
        placing, flat_in, (((0,), (0,)), ((), ())), preferred_element_type=jnp.float32
    )
    buffer = buffer.astype(jnp.bfloat16).reshape(EXP, CAP, width)
    weights = jax.nn.softmax(gate_logits, axis=-1)
    mixing = weights[:, 0:1] * first_hit.astype(jnp.float32) + weights[:, 1:2] * second_hit.astype(
        jnp.float32
    )
    moved_rows, moved_high = from_behind((buffer, flat_h[:, half:]), "sec", 1)
    mine = lax.dynamic_index_in_dim(
        lax.all_gather(moved_rows, "dev", axis=1, tiled=True), my_expert, 0, keepdims=False
    )
    partials = lax.cond(
        is_expert,
        lambda block: expert_rows(block, w_gate, w_up, w_down),
        lambda block: jnp.zeros_like(block),
        mine,
    )
    partials = partials.reshape(devices, CAP, width)
    returned = lax.all_to_all(partials, "dev", split_axis=0, concat_axis=0, tiled=True)
    summed = jnp.sum(returned.reshape(EXP, group, CAP, width).astype(jnp.float32), axis=1)
    mixed = jnp.dot(
        mixing,
        summed.reshape(EXP * CAP, width),
        precision=lax.Precision.HIGHEST,
        preferred_element_type=jnp.float32,
    )
    upper_out = (moved_high.astype(jnp.float32) + mixed[:, half:]).astype(jnp.bfloat16)
    lower_mix = from_behind(mixed[:, :half], "sec", -1)
    lower_out = (flat_h[:, :half].astype(jnp.float32) + lower_mix).astype(jnp.bfloat16)
    layer_out = jnp.where(is_attention, lower_out, upper_out)
    return layer_out.reshape(requests, steps, half)


def solution(mesh):
    return jax.shard_map(
        shards,
        mesh=mesh,
        in_specs=(
            P("dev", None, None),
            P("dev", None, None),
            P("dev", None, None),
            P("dev"),
            P("dev", None, None),
            P("dev", None, None),
            P("dev", None, None),
            P(),
            P("dev", None),
            P("dev", None),
            P(None, "dev"),
            P(None, "dev"),
            P("dev", None),
        ),
        out_specs=P("dev", None, "sec"),
        check_vma=False,
    )
```

profile of v0, /device:TPU:25, one launch (start us, length us, event | category | flops | bytes accessed | tf_op | source)
XLA Modules:
  0.0 403.3 jit_solution(4926750830387768052)
XLA Ops:
  6.5 0.8 copy.52
  7.3 0.1 eq.49
  7.4 0.1 fusion.29
  7.5 0.2 select_reduce_fusion
  7.7 0.1 reduce_sum.48
  7.8 0.1 copy.53
  7.9 0.7 multiply_add_fusion
  8.6 0.8 conditional.2
  8.6 0.7 broadcast.102
  9.3 0.4 convolution_convert_fusion.1
  9.7 0.2 reshape.122
  9.9 0.4 copy.54
  10.3 1.3 collective-permute-start
  11.6 11.2 %collective-permute-done = bf16[4,9,6144]{2,0,1:T(4,128)(2,1)S(1)} collective-permute-done((bf16[4,9,6144]{2,0,1:T(4,128)(2,1)S(1)}, bf16[4,9,6144]{2,0,1:T(4,128)(2,1)S(1)}, u32[]{:S(2)}, u32[]{:S(2)}) %collective-permute-start) | collective-permute-done | bytes 442400 | tf_op jit(solution)/shard_map/ppermute | solution.py:18
  22.8 0.8 copy-done
  23.6 144.2 %all-gather.2.cloned.1.call-done = bf16[4,576,6144]{2,0,1:T(4,128)(2,1)} async-done(((bf16[4,9,6144]{2,0,1:T(4,128)(2,1)}), bf16[4,576,6144]{2,0,1:T(4,128)(2,1)}) %all-gather.2.cloned.1.call-update) | async-done | bytes 28311568 | tf_op jit(solution)/shard_map/all_gather | solution.py:124
  167.8 41.2 %conditional.3 = (bf16[576,6144]{1,0:T(8,128)(2,1)}) conditional(s32[]{:T(128)} %convert_element_type.63, () %tuple.38, (s32[]{:T(128)}, s32[]{:T(128)}, s32[]{:T(128)}, bf16[4,576,6144]{2,0,1:T(4,128)(2,1)}, bf16[6144,512]{1,0:T(8,128)(2,1)}, /*index=5*/bf16[6144,512]{1,0:T(8,128)(2,1)}, bf16[512,6144]{1,0:T(8,128)(2,1)}, s32[]{:T(128)}) %tuple.40), branch_computations={%region_9.10_spmd, %region_10.11_spmd.clone} | conditional | flops 10876944384 | bytes 144310560 | solution.py:126
  167.8 20.3 %copy.55 = bf16[4,576,6144]{2,1,0:T(8,128)(2,1)} copy(bf16[4,576,6144]{2,0,1:T(4,128)(2,1)} %get-tuple-element.212) | data formatting | bytes 56623104 | tf_op jit(solution)/shard_map
  188.1 8.0 %fusion.15 = f32[576,512]{1,0:T(8,128)S(1)} fusion(bf16[6144,512]{1,0:T(8,128)(2,1)} %get-tuple-element.190, bf16[4,576,6144]{2,1,0:T(8,128)(2,1)} %copy.55, s32[]{:T(128)S(6)} %select_n.31), kind=kOutput, calls=%fused_computation.30 | convolution fusion | flops 3623878656 | bytes 14548996 | tf_op jit(solution)/shard_map/cond/branch_1_fun/dot_general | solution.py:61
  196.1 6.9 %fusion.22 = bf16[576,512]{1,0:T(8,128)(2,1)S(1)} fusion(bf16[6144,512]{1,0:T(8,128)(2,1)S(1)} %copy-done.5, bf16[4,576,6144]{2,1,0:T(8,128)(2,1)} %copy.55, s32[]{:T(128)S(6)} %select_n.31, f32[576,512]{1,0:T(8,128)S(1)} %fusion.15), kind=kOutput, calls=%fused_computation.35 | convolution fusion | flops 3625648128 | bytes 15138820 | tf_op jit(solution)/shard_map/cond/branch_1_fun/dot_general | solution.py:62
  203.1 6.0 %convolution_convert_fusion = bf16[576,6144]{1,0:T(8,128)(2,1)} fusion(bf16[576,512]{1,0:T(8,128)(2,1)S(1)} %fusion.22, bf16[512,6144]{1,0:T(8,128)(2,1)S(1)} %bitcast.39), kind=kOutput, calls=%fused_computation.27 | convolution fusion | flops 3627417600 | bytes 13959168 | tf_op jit(solution)/shard_map/cond/branch_1_fun/dot_general | solution.py:64
  209.0 10.2 %reshape.123 = bf16[64,9,6144]{2,1,0:T(8,128)(2,1)} reshape(bf16[576,6144]{1,0:T(8,128)(2,1)} %get-tuple-element.235) | data formatting | bytes 14155776 | tf_op jit(solution)/shard_map/reshape | solution.py:132
  219.3 8.4 %all-to-all-start = ((bf16[64,9,6144]{2,1,0:T(8,128)(2,1)}), bf16[64,9,6144]{2,1,0:T(8,128)(2,1)}, u32[]{:S(2)}, u32[]{:S(2)}) async-start(bf16[64,9,6144]{2,1,0:T(8,128)(2,1)} %reshape.123), calls=%async_computation | async-start | bytes 25165824 | tf_op jit(solution)/shard_map/all_to_all | solution.py:133
  227.8 154.7 %all-to-all-done = bf16[64,9,6144]{2,1,0:T(8,128)(2,1)} async-done(((bf16[64,9,6144]{2,1,0:T(8,128)(2,1)}), bf16[64,9,6144]{2,1,0:T(8,128)(2,1)}, u32[]{:S(2)}, u32[]{:S(2)}) %all-to-all-start) | async-done | bytes 7077920 | tf_op jit(solution)/shard_map/all_to_all | solution.py:133
  382.5 6.8 %convert_reduce_fusion = f32[4,9,6144]{2,1,0:T(8,128)S(1)} fusion(bf16[64,9,6144]{2,1,0:T(8,128)(2,1)} %all-to-all-done), kind=kLoop, calls=%fused_computation.38 | loop fusion | flops 6856704 | bytes 7962624 | tf_op jit(solution)/shard_map/reduce_sum | solution.py:134
  389.3 0.1 reshape.124
  389.5 0.7 fusion.30
  390.2 1.3 collective-permute-start.1
  391.5 1.0 reshape.121
  392.5 1.3 collective-permute-start.2
  393.8 1.9 collective-permute-done.2
  395.7 0.7 reshape.125
  (23 shorter events, 0.2 us)
Async XLA Ops:
  6.5 161.3 %all-gather.2.cloned.1.call-start = ((), (), s32[]{:S(2)}) async-start(), calls=%async_computation.1 | async-start | bytes 28753920 | tf_op jit(solution)/shard_map/all_gather | solution.py:124
  10.3 12.5 %collective-permute-start = (bf16[4,9,6144]{2,0,1:T(4,128)(2,1)S(1)}, bf16[4,9,6144]{2,0,1:T(4,128)(2,1)S(1)}, u32[]{:S(2)}, u32[]{:S(2)}) collective-permute-start(bf16[4,9,6144]{2,0,1:T(4,128)(2,1)S(1)} %copy.54), channel_id=1, source_target_pairs={{0,64},{1,65},{2,66},{3,67},{4,68},{5,69},{6,70},{7,71},{8,72},{9,... | collective-permute-start | bytes 1327112 | tf_op jit(solution)/shard_map/ppermute | solution.py:18
  22.8 0.8 copy-start
  167.8 35.2 %slice-start = ((s8[6291456]{0:T(1024)(128)(4,1)}), s8[2097152]{0:T(1024)(128)(4,1)S(1)}, s32[]{:S(2)}) async-start(s8[6291456]{0:T(1024)(128)(4,1)} %bitcast.38), calls=%async_computation.2 | async-start | bytes 4194304 | tf_op jit(solution)/shard_map/cond
  188.1 8.0 %copy-start.5 = (bf16[6144,512]{1,0:T(8,128)(2,1)S(1)}, bf16[6144,512]{1,0:T(8,128)(2,1)}, u32[]{:S(2)}) copy-start(bf16[6144,512]{1,0:T(8,128)(2,1)} %get-tuple-element.191) | copy-start | bytes 18874372 | tf_op jit(solution)/shard_map/cond
  188.1 15.0 %slice-start.1 = ((s8[6291456]{0:T(1024)(128)(4,1)}), s8[4194304]{0:T(1024)(128)(4,1)S(1)}, s32[]{:S(2)}) async-start(s8[6291456]{0:T(1024)(128)(4,1)} %bitcast.38), calls=%async_computation.3 | async-start | bytes 8388608 | tf_op jit(solution)/shard_map/cond
  219.3 8.4 %copy-start.4 = (f32[16,2]{0,1:T(2,128)S(1)}, f32[16,2]{0,1:T(2,128)}, u32[]{:S(2)}) copy-start(f32[16,2]{0,1:T(2,128)} %param.26) | copy-start | bytes 388
  219.3 163.2 %all-to-all-start = ((bf16[64,9,6144]{2,1,0:T(8,128)(2,1)}), bf16[64,9,6144]{2,1,0:T(8,128)(2,1)}, u32[]{:S(2)}, u32[]{:S(2)}) async-start(bf16[64,9,6144]{2,1,0:T(8,128)(2,1)} %reshape.123), calls=%async_computation | async-start | bytes 25165824 | tf_op jit(solution)/shard_map/all_to_all | solution.py:133
  390.2 5.5 %collective-permute-start.1 = (f32[16,3072]{1,0:T(8,128)S(1)}, f32[16,3072]{1,0:T(8,128)S(1)}, u32[]{:S(2)}, u32[]{:S(2)}) collective-permute-start(f32[16,3072]{1,0:T(8,128)S(1)} %slice.33), channel_id=1, source_target_pairs={{64,0},{65,1},{66,2},{67,3},{68,4},{69,5},{70,6},{71,7},{72,8},{73... | collective-permute-start | bytes 589832 | tf_op jit(solution)/shard_map/ppermute | solution.py:18
  392.5 3.2 collective-permute-start.2
Sparse Core Ops, SparseCore 0:
  23.7 144.0 all-gather.1
where the time goes:
time: 404 us; the launch traced here: 403 us
  waiting for transfers between devices  312 us (77%)
  local copies, waits for them, and re-layouts  35.4 us (9%)
  matrix products  22 us (5%)
  between operations  13.5 us (3%)
  starting transfers between devices  12.3 us (3%)
  other arithmetic  7.96 us (2%)
    all_to_all x1, waiting for transfers between devices, shards(): lax.all_to_all(partials, 'dev', split_axis=0, concat_axis=0, tiled=True)  155 us
    all_gather x1, waiting for transfers between devices, shards(): lax.all_gather(moved_rows, 'dev', axis=1, tiled=True)  144 us
    another operation x2, local copies, waits for them, and re-layouts  21 us
    ppermute x3, waiting for transfers between devices, from_behind(): return lax.ppermute(x, axis, pairs)  13.1 us
    reshape x1, local copies, waits for them, and re-layouts, shards(): partials = partials.reshape(devices, CAP, width)  10.2 us
    all_to_all x1, starting transfers between devices, shards(): lax.all_to_all(partials, 'dev', split_axis=0, concat_axis=0, tiled=True)  8.42 us
  transfers between devices with their start and end apart: 5, of which 4 were waited for; matrix products, arithmetic and copies ran while one was open for 0% of the time, Pallas kernels for 0%

commit v1 on v0

--- a/solution.py
+++ b/solution.py
@@ -121,7 +121,12 @@
     )
     moved_rows, moved_high = from_behind((buffer, flat_h[:, half:]), "sec", 1)
     mine = lax.dynamic_index_in_dim(
-        lax.all_gather(moved_rows, "dev", axis=1, tiled=True), my_expert, 0, keepdims=False
+        jnp.concatenate(
+            lax.all_to_all(jnp.stack([moved_rows] * lax.axis_size("dev")), "dev", 0, 0), axis=1
+        ),
+        my_expert,
+        0,
+        keepdims=False,
     )
     partials = lax.cond(
         is_expert,

time: 404 us -> 815 us (2.02); the launches traced: 403 us -> 805 us
  waiting for transfers between devices: 312 us -> 671 us
  starting transfers between devices: 12.3 us -> 59.3 us
  between operations: 13.5 us -> 0.15 us
  local copies, waits for them, and re-layouts: 35.4 us -> 46.4 us
    all_to_all x0 -> x1, waiting for transfers between devices: none -> 500 us  [shards(): lax.all_to_all(jnp.stack([moved_rows] * lax.axis_size('dev')), 'dev', 0, 0)]
    all_gather x1 -> x0, waiting for transfers between devices: 144 us -> none  [shards(): lax.all_gather(moved_rows, 'dev', axis=1, tiled=True)]
    all_to_all x1, starting transfers between devices: 8.42 us -> 44.6 us  [shards(): lax.all_to_all(partials, 'dev', split_axis=0, concat_axis=0, tiled=True)]
    dynamic_slice x0 -> x1, local copies, waits for them, and re-layouts: none -> 17 us  [shards(): lax.dynamic_index_in_dim(jnp.concatenate(lax.all_to_all(jnp.stack([moved_...]
    all_to_all x0 -> x1, starting transfers between devices: none -> 10.8 us  [shards(): lax.all_to_all(jnp.stack([moved_rows] * lax.axis_size('dev')), 'dev', 0, 0)]
where the time goes in v1:
time: 815 us; the launch traced here: 805 us
  waiting for transfers between devices  671 us (82%)
  starting transfers between devices  59.3 us (7%)
  local copies, waits for them, and re-layouts  46.4 us (6%)
  matrix products  19.7 us (2%)
    all_to_all x1, waiting for transfers between devices, shards(): lax.all_to_all(jnp.stack([moved_rows] * lax.axis_size('dev')), 'dev', 0, 0)  500 us
    all_to_all x1, waiting for transfers between devices, shards(): lax.all_to_all(partials, 'dev', split_axis=0, concat_axis=0, tiled=True)  158 us
    all_to_all x1, starting transfers between devices, shards(): lax.all_to_all(partials, 'dev', split_axis=0, concat_axis=0, tiled=True)  44.6 us
    dynamic_slice x1, local copies, waits for them, and re-layouts, shards(): lax.dynamic_index_in_dim(jnp.concatenate(lax.all_to_all(jnp.stack([moved_...  17 us
  transfers between devices with their start and end apart: 5, of which 4 were waited for; matrix products, arithmetic and copies ran while one was open for 0% of the time, Pallas kernels for 0%

profile of v1, /device:TPU:25, one launch (start us, length us, event | category | flops | bytes accessed | tf_op | source)
XLA Modules:
  0.0 804.5 jit_solution(16311713717833972563)
XLA Ops:
  0.0 0.8 copy.60
  0.8 0.1 eq.49
  1.0 0.2 select_reduce_fusion
  1.2 0.1 reduce_sum.48
  1.2 0.1 copy.61
  1.3 0.7 multiply_add_fusion
  2.0 0.8 conditional.2
  2.0 0.7 broadcast.104
  2.8 0.4 convolution_convert_fusion.1
  3.2 0.2 reshape.134
  3.4 0.4 copy.62
  3.8 1.3 collective-permute-start
  5.1 10.6 %collective-permute-done = bf16[4,9,6144]{2,0,1:T(4,128)(2,1)S(1)} collective-permute-done((bf16[4,9,6144]{2,0,1:T(4,128)(2,1)S(1)}, bf16[4,9,6144]{2,0,1:T(4,128)(2,1)S(1)}, u32[]{:S(2)}, u32[]{:S(2)}) %collective-permute-start) | collective-permute-done | bytes 442400 | tf_op jit(solution)/shard_map/ppermute | solution.py:18
  15.6 15.0 %stack.2 = bf16[64,4,9,6144]{3,1,2,0:T(4,128)(2,1)} broadcast(bf16[4,9,6144]{2,0,1:T(4,128)(2,1)S(1)} %collective-permute-done), dimensions={1,2,3} | broadcast | bytes 28753920 | tf_op jit(solution)/shard_map/stack | solution.py:125
  30.6 10.8 %all-to-all-start = ((bf16[64,4,9,6144]{3,1,2,0:T(4,128)(2,1)}), bf16[64,4,9,6144]{3,1,2,0:T(4,128)(2,1)}, u32[]{:S(2)}, u32[]{:S(2)}) async-start(bf16[64,4,9,6144]{3,1,2,0:T(4,128)(2,1)} %stack.2), calls=%async_computation | async-start | bytes 56623104 | tf_op jit(solution)/shard_map/all_to_all | solution.py:125
  41.4 500.4 %all-to-all-done = bf16[64,4,9,6144]{3,1,2,0:T(4,128)(2,1)} async-done(((bf16[64,4,9,6144]{3,1,2,0:T(4,128)(2,1)}), bf16[64,4,9,6144]{3,1,2,0:T(4,128)(2,1)}, u32[]{:S(2)}, u32[]{:S(2)}) %all-to-all-start) | async-done | bytes 28311584 | tf_op jit(solution)/shard_map/all_to_all | solution.py:125
  541.8 35.7 %conditional.3 = (bf16[576,6144]{1,0:T(8,128)(2,1)}) conditional(s32[]{:T(128)} %convert_element_type.63, () %tuple.38, (bf16[4,64,9,6144]{3,0,2,1:T(4,128)(2,1)}, s32[]{:T(128)}, s32[]{:T(128)}, s32[]{:T(128)}, bf16[6144,512]{1,0:T(8,128)(2,1)}, /*index=5*/bf16[6144,512]{1,0:T(8,128)(2,1)}, bf16[512,6144]{1,0:T(8,128)(2,1)}, s32[]{:T(128)}) %tuple.40), branch_computations={%region_9.10_spmd, %region_10.11_spmd.clone} | conditional | flops 10876944384 | bytes 101843216 | solution.py:131
  541.8 17.0 %constant_dynamic-slice_fusion = bf16[1,576,6144]{2,0,1:T(2,128)(2,1)S(1)} fusion(bf16[4,576,6144]{2,0,1:T(4,128)(2,1)} %bitcast.10, s32[]{:T(128)S(6)} %select_n.31), kind=kLoop, calls=%fused_computation.36 | loop fusion | bytes 14155780 | tf_op jit(solution)/shard_map/jit(dynamic_index_in_dim)/dynamic_slice | solution.py:123
  558.8 5.2 fusion.15
  564.0 7.6 fusion.22
  571.7 5.8 convolution_convert_fusion
  577.5 10.2 %reshape.136 = bf16[64,9,6144]{2,1,0:T(8,128)(2,1)} reshape(bf16[576,6144]{1,0:T(8,128)(2,1)} %get-tuple-element.220) | data formatting | bytes 14155776 | tf_op jit(solution)/shard_map/reshape | solution.py:137
  587.7 44.6 %all-to-all-start.1 = ((bf16[64,9,6144]{2,1,0:T(8,128)(2,1)}), bf16[64,9,6144]{2,1,0:T(8,128)(2,1)}, u32[]{:S(2)}, u32[]{:S(2)}) async-start(bf16[64,9,6144]{2,1,0:T(8,128)(2,1)} %reshape.136), calls=%async_computation.1 | async-start | bytes 25165824 | tf_op jit(solution)/shard_map/all_to_all | solution.py:138
  632.4 158.2 %all-to-all-done.1 = bf16[64,9,6144]{2,1,0:T(8,128)(2,1)} async-done(((bf16[64,9,6144]{2,1,0:T(8,128)(2,1)}), bf16[64,9,6144]{2,1,0:T(8,128)(2,1)}, u32[]{:S(2)}, u32[]{:S(2)}) %all-to-all-start.1) | async-done | bytes 7077920 | tf_op jit(solution)/shard_map/all_to_all | solution.py:138
  790.6 6.8 convert_reduce_fusion
  797.5 0.1 reshape.137
  797.6 0.7 fusion.28
  798.3 1.3 collective-permute-start.1
  799.6 1.0 reshape.133
  800.6 1.3 collective-permute-start.2
  801.9 1.9 collective-permute-done.2
  803.8 0.7 reshape.138
  (21 shorter events, 0.3 us)
Async XLA Ops:
  3.8 11.8 %collective-permute-start = (bf16[4,9,6144]{2,0,1:T(4,128)(2,1)S(1)}, bf16[4,9,6144]{2,0,1:T(4,128)(2,1)S(1)}, u32[]{:S(2)}, u32[]{:S(2)}) collective-permute-start(bf16[4,9,6144]{2,0,1:T(4,128)(2,1)S(1)} %copy.62), channel_id=1, source_target_pairs={{0,64},{1,65},{2,66},{3,67},{4,68},{5,69},{6,70},{7,71},{8,72},{9,... | collective-permute-start | bytes 1327112 | tf_op jit(solution)/shard_map/ppermute | solution.py:18
  30.6 511.2 %all-to-all-start = ((bf16[64,4,9,6144]{3,1,2,0:T(4,128)(2,1)}), bf16[64,4,9,6144]{3,1,2,0:T(4,128)(2,1)}, u32[]{:S(2)}, u32[]{:S(2)}) async-start(bf16[64,4,9,6144]{3,1,2,0:T(4,128)(2,1)} %stack.2), calls=%async_computation | async-start | bytes 56623104 | tf_op jit(solution)/shard_map/all_to_all | solution.py:125
  541.8 17.0 %copy-start.4 = (bf16[6144,512]{1,0:T(8,128)(2,1)S(1)}, bf16[6144,512]{1,0:T(8,128)(2,1)}, u32[]{:S(2)}) copy-start(bf16[6144,512]{1,0:T(8,128)(2,1)} %get-tuple-element.191) | copy-start | bytes 18874372 | tf_op jit(solution)/shard_map/cond
  558.8 12.9 %slice-start = ((s8[6291456]{0:T(1024)(128)(4,1)}), s8[2097152]{0:T(1024)(128)(4,1)S(1)}, s32[]{:S(2)}) async-start(s8[6291456]{0:T(1024)(128)(4,1)} %bitcast.40), calls=%async_computation.2 | async-start | bytes 4194304 | tf_op jit(solution)/shard_map/cond
  564.0 7.7 slice-start.1
  587.7 44.6 %copy-start.3 = (f32[16,2]{0,1:T(2,128)S(1)}, f32[16,2]{0,1:T(2,128)}, u32[]{:S(2)}) copy-start(f32[16,2]{0,1:T(2,128)} %param.26) | copy-start | bytes 388
  587.7 202.9 %all-to-all-start.1 = ((bf16[64,9,6144]{2,1,0:T(8,128)(2,1)}), bf16[64,9,6144]{2,1,0:T(8,128)(2,1)}, u32[]{:S(2)}, u32[]{:S(2)}) async-start(bf16[64,9,6144]{2,1,0:T(8,128)(2,1)} %reshape.136), calls=%async_computation.1 | async-start | bytes 25165824 | tf_op jit(solution)/shard_map/all_to_all | solution.py:138
  798.3 5.5 collective-permute-start.1
  800.6 3.2 collective-permute-start.2
